TPU v7x, 32 devices: a whole 2x2x4 slice. The times are simulated.
32 devices in a mesh: row: 8 (over z, y), col: 4 (over x, core).
Axes of the slice: x: 2, y: 2, z: 4, core: 2. Of those that a mesh axis runs over, the one named last changes fastest.
Arguments:
- left_act: bfloat16 [768, 128], P(('row', 'col')), may hold values from -540 to 540
- right_act: bfloat16 [768, 128], P(('row', 'col')), may hold values from -6 to 6
- norm_gain: float32 [128], replicated, may hold values from 0.25 to 1.75
- norm_bias: float32 [128], replicated, may hold values from -3 to 3
- w_in: bfloat16 [128, 512], replicated, may hold values from -0.5 to 0.5
- b_in: float32 [512], replicated, may hold values from -3 to 3
- w_out: bfloat16 [512, 128], replicated, may hold values from -0.25 to 0.25
- w_bins: bfloat16 [128, 64], replicated, may hold values from -0.5 to 0.5
- labels: int32 [768, 768], P('row', 'col'), may hold values from 0 to 63, as said below
Outputs:
- grad_left: float32 [768, 128], P(('row', 'col'))
- grad_right: float32 [768, 128], P('col')
- grad_w_in: float32 [128, 512], replicated
- grad_w_out: float32 [512, 128], replicated
- grad_w_bins: float32 [128, 64], replicated
Inputs may be any that keep to these rules, and one draw needn't show every extreme that they name: labels is symmetric: labels[i, j] equals labels[j, i].
All inputs are finite; a program needn't handle non-finite values.
Results may differ from a plain program's by a relative error of at most 0.00039.
Values may be sent and summed in bfloat16 or wider, within the bound.
A program may use at most 64 MiB of HBM per device.

v0:
```python
import jax
import jax.numpy as jnp
from jax import lax
from jax.sharding import PartitionSpec as P


def inner(first, second):
    return lax.dot_general(
        first, second, (((0,), (0,)), ((), ())), preferred_element_type=jnp.float32
    )


def outer(first, second):
    return lax.dot_general(
        first, second, (((1,), (1,)), ((), ())), preferred_element_type=jnp.float32
    )


def transition(left_rows, right_cols, gain, bias, w_in, b_in, w_out):
    summed = (
        left_rows.astype(jnp.float32)[:, None, :] + right_cols.astype(jnp.float32)[None, :, :]
    ).reshape(-1, left_rows.shape[1])
    center = summed - jnp.mean(summed, axis=-1, keepdims=True)
    inv_scale = lax.rsqrt(jnp.mean(center * center, axis=-1, keepdims=True) + 1e-05)
    normal_form = center * inv_scale
    normed = (normal_form * gain + bias).astype(jnp.bfloat16)
    pre_act = jnp.dot(normed, w_in, preferred_element_type=jnp.float32) + b_in
    hidden = (pre_act * jax.nn.sigmoid(pre_act)).astype(jnp.bfloat16)
    updated = (summed + jnp.dot(hidden, w_out, preferred_element_type=jnp.float32)).astype(
        jnp.bfloat16
    )
    return (normal_form, inv_scale, normed, pre_act, hidden, updated)


def pair_backward(sym, bin_labels, parts, gain, w_in, w_out, w_bins):
    normal_form, inv_scale, normed, pre_act, hidden, updated = parts
    shifted = sym - jnp.max(sym, axis=-1, keepdims=True)
    expo = jnp.exp(shifted)
    probs = expo / jnp.sum(expo, axis=-1, keepdims=True)
    onehot = (bin_labels[..., None] == lax.iota(jnp.int32, sym.shape[-1])).astype(jnp.float32)
    logit_grad = (2.0 * (probs - onehot)).reshape(-1, sym.shape[-1]).astype(jnp.bfloat16)
    grad_bins = inner(updated, logit_grad)
    upd_grad = outer(logit_grad, w_bins)
    upd_half = upd_grad.astype(jnp.bfloat16)
    grad_out = inner(hidden, upd_half)
    hid_grad = outer(upd_half, w_out)
    sigma = jax.nn.sigmoid(pre_act)
    pre_grad = (hid_grad * sigma * (1.0 + pre_act * (1.0 - sigma))).astype(jnp.bfloat16)
    grad_in = inner(normed, pre_grad)
    norm_grad = outer(pre_grad, w_in) * gain
    pair_grad = (
        inv_scale
        * (
            norm_grad
            - jnp.mean(norm_grad, axis=-1, keepdims=True)
            - normal_form * jnp.mean(norm_grad * normal_form, axis=-1, keepdims=True)
        )
        + upd_grad
    )
    return (grad_in, grad_out, grad_bins, pair_grad)


def on_device(left_act, right_act, norm_gain, norm_bias, w_in, b_in, w_out, w_bins, labels):
    tile_rows, tile_cols = labels.shape
    width = left_act.shape[1]
    stacked = jnp.stack([left_act, right_act])
    everything = lax.all_gather(stacked, ("row", "col"), axis=1, tiled=True)
    row_block = lax.dynamic_slice_in_dim(
        everything, lax.axis_index("row") * tile_rows, tile_rows, 1
    )
    column_block = lax.dynamic_slice_in_dim(
        everything, lax.axis_index("col") * tile_cols, tile_cols, 1
    )
    stride_rows = 8
    groups = tile_rows // stride_rows

    def advance(running, record):
        left_rows, right_rows, bin_labels = record
        own_parts = transition(left_rows, column_block[1], norm_gain, norm_bias, w_in, b_in, w_out)
        own_logits = jnp.dot(own_parts[5], w_bins, preferred_element_type=jnp.float32).reshape(
            stride_rows, tile_cols, -1
        )
        far_parts = transition(column_block[0], right_rows, norm_gain, norm_bias, w_in, b_in, w_out)
        far_logits = jnp.dot(far_parts[5], w_bins, preferred_element_type=jnp.float32).reshape(
            tile_cols, stride_rows, -1
        )
        sym = own_logits + jnp.transpose(far_logits, (1, 0, 2))
        grads = pair_backward(sym, bin_labels, own_parts, norm_gain, w_in, w_out, w_bins)
        pair_grad = grads[3].reshape(stride_rows, tile_cols, width)
        running = (
            running[0] + grads[0],
            running[1] + grads[1],
            running[2] + grads[2],
            running[3] + jnp.sum(pair_grad, axis=0),
        )
        return (running, jnp.sum(pair_grad, axis=1))

    start = (
        jnp.zeros((width, w_in.shape[1]), jnp.float32),
        jnp.zeros((w_in.shape[1], width), jnp.float32),
        jnp.zeros((width, w_bins.shape[1]), jnp.float32),
        jnp.zeros((tile_cols, width), jnp.float32),
    )
    records = (
        row_block[0].reshape(groups, stride_rows, width),
        row_block[1].reshape(groups, stride_rows, width),
        labels.reshape(groups, stride_rows, tile_cols),
    )
    running, left_terms = lax.scan(advance, start, records)
    grad_left = lax.psum_scatter(
        left_terms.reshape(tile_rows, width), "col", scatter_dimension=0, tiled=True
    )
    grad_right = lax.psum(running[3], "row")
    grad_in, grad_out, grad_bins = lax.psum((running[0], running[1], running[2]), ("row", "col"))
    residues = tile_rows * lax.axis_size("row")
    return (grad_left, grad_right, grad_in / residues, grad_out / residues, grad_bins / residues)


def solution(mesh):
    placed = (
        P(("row", "col"), None),
        P(("row", "col"), None),
        P(),
        P(),
        P(),
        P(),
        P(),
        P(),
        P("row", "col"),
    )
    return jax.shard_map(
        on_device,
        mesh=mesh,
        in_specs=placed,
        out_specs=(P(("row", "col"), None), P("col", None), P(), P(), P()),
        check_vma=False,
    )
```

profile of v0, /device:TPU:0, one launch (start us, length us, event | category | flops | bytes accessed | tf_op | source)
XLA Modules:
  0.0 632.4 jit_solution(9450483110087516917)
XLA Ops:
  8.8 44.3 %all_gather.3 = bf16[2,768,128]{2,1,0:T(8,128)(2,1)S(1)} all-gather(bf16[2,24,128]{2,1,0:T(8,128)(2,1)S(1)} %pad_maximum_fusion), channel_id=1, replica_groups=mesh['row'=8,'col'=4] {'row','col'}, dimensions={1}, use_global_device_ids=true | all-gather | bytes 405504 | tf_op jit(solution)/shard_map/all_gather | solution.py:67
  54.4 369.4 %while.19 = (s32[]{:T(128)}, f32[128,512]{1,0:T(8,128)}, f32[512,128]{1,0:T(8,128)S(1)}, f32[128,64]{0,1:T(8,128)}, f32[192,128]{1,0:T(8,128)}, /*index=5*/f32[1...) while((s32[]{:T(128)}, f32[128,512]{1,0:T(8,128)}, ...), condition=%wide.region_11.12_spmd.clone, body=%wide.region_0.11_spmd.clone.sunk | while | flops 1737784448 | bytes 44289180 | solution.py:109
  58.9 3.2 fusion.120
  63.3 2.6 multiply_convert_fusion.3
  69.9 5.1 fusion.121
  77.1 3.5 fusion.123
  89.7 3.2 fusion.120
  94.1 2.6 multiply_convert_fusion.3
  100.7 5.1 fusion.121
  105.7 1.4 copy.32
  107.9 3.5 fusion.123
  120.5 3.2 fusion.120
  124.9 2.6 multiply_convert_fusion.3
  131.5 5.1 fusion.121
  136.5 1.4 copy.32
  138.7 3.5 fusion.123
  151.3 3.2 fusion.120
  155.7 2.6 multiply_convert_fusion.3
  162.3 5.1 fusion.121
  167.3 1.4 copy.32
  169.5 3.5 fusion.123
  182.1 3.2 fusion.120
  186.5 2.6 multiply_convert_fusion.3
  193.0 5.1 fusion.121
  198.1 1.4 copy.32
  200.3 3.5 fusion.123
  212.8 3.2 fusion.120
  217.3 2.6 multiply_convert_fusion.3
  223.8 5.1 fusion.121
  228.9 1.4 copy.32
  231.1 3.5 fusion.123
  243.6 3.2 fusion.120
  248.1 2.6 multiply_convert_fusion.3
  254.6 5.1 fusion.121
  259.7 1.4 copy.32
  261.9 3.5 fusion.123
  274.4 3.2 fusion.120
  278.9 2.6 multiply_convert_fusion.3
  285.4 5.1 fusion.121
  292.6 3.5 fusion.123
  305.2 3.2 fusion.120
  309.6 2.6 multiply_convert_fusion.3
  316.2 5.1 fusion.121
  321.2 1.4 copy.32
  323.4 3.5 fusion.123
  336.0 3.2 fusion.120
  340.4 2.6 multiply_convert_fusion.3
  346.9 5.1 fusion.121
  352.0 1.4 copy.32
  354.2 3.5 fusion.123
  366.7 3.2 fusion.120
  371.2 2.6 multiply_convert_fusion.3
  377.7 5.1 fusion.121
  385.0 3.5 fusion.123
  397.5 3.2 fusion.120
  402.0 2.6 multiply_convert_fusion.3
  408.5 5.1 fusion.121
  415.8 3.5 fusion.123
  425.9 37.2 %psum.31 = f32[128,64]{0,1:T(8,128)S(1)} all-reduce(f32[128,64]{0,1:T(8,128)} %get-tuple-element.95), channel_id=1, replica_groups=mesh['row'=8,'col'=4] {'row','col'}, use_global_device_ids=true, to_apply=%region_16.17 | all-reduce | flops 8192 | bytes 65536 | tf_op jit(solution)/shard_map/psum | solution.py:114
  463.7 86.6 %all-reduce.7.cloned.1.call-done = (f32[128,512]{1,0:T(8,128)}, f32[512,128]{1,0:T(8,128)}) async-done(((f32[128,512]{1,0:T(8,128)}, f32[512,128]{1,0:T(8,128)}), (f32[128,512]{1,0:T(8,128)}, f32[512,128]{1,0:T(8,128)})) %all-reduce.7.cloned.1.call-update) | async-done | bytes 524304 | tf_op jit(solution)/shard_map/psum | solution.py:114
  550.3 1.7 broadcast_multiply_fusion.5
  552.0 1.7 broadcast_multiply_fusion.4
  553.7 69.8 %all-reduce.5.cloned.1.call-done = f32[192,128]{1,0:T(8,128)} async-done(((f32[192,128]{1,0:T(8,128)}), f32[192,128]{1,0:T(8,128)}) %all-reduce.5.cloned.1.call-update) | async-done | bytes 98320 | tf_op jit(solution)/shard_map/psum | solution.py:113
  623.4 1.5 copy.55
  (826 shorter events, 186.1 us)
Async XLA Ops:
  8.0 542.3 %all-reduce.7.cloned.1.call-start = ((), (), s32[]{:S(2)}) async-start(), calls=%async_computation.3 | async-start | bytes 1048576 | tf_op jit(solution)/shard_map/psum | solution.py:114
  58.9 4.4 copy-start.7
  58.9 4.4 copy-start.17
  69.9 6.7 %copy-start.12 = (f32[128,64]{0,1:T(8,128)S(1)}, f32[128,64]{0,1:T(8,128)}, u32[]{:S(2)}) copy-start(f32[128,64]{0,1:T(8,128)} %get-tuple-element.372) | copy-start | bytes 98308 | tf_op jit(solution)/shard_map/while
  69.9 6.9 %copy-start.11 = (bf16[128,64]{0,1:T(8,128)(2,1)S(1)}, bf16[128,64]{0,1:T(8,128)(2,1)}, u32[]{:S(2)}) copy-start(bf16[128,64]{0,1:T(8,128)(2,1)} %get-tuple-element.400) | copy-start | bytes 49156 | tf_op jit(solution)/shard_map/while
  77.1 4.2 copy-start.3
  89.6 4.4 copy-start.7
  89.7 4.4 copy-start.17
  100.6 6.7 %copy-start.12 = (f32[128,64]{0,1:T(8,128)S(1)}, f32[128,64]{0,1:T(8,128)}, u32[]{:S(2)}) copy-start(f32[128,64]{0,1:T(8,128)} %get-tuple-element.372) | copy-start | bytes 98308 | tf_op jit(solution)/shard_map/while
  100.7 6.9 %copy-start.11 = (bf16[128,64]{0,1:T(8,128)(2,1)S(1)}, bf16[128,64]{0,1:T(8,128)(2,1)}, u32[]{:S(2)}) copy-start(bf16[128,64]{0,1:T(8,128)(2,1)} %get-tuple-element.400) | copy-start | bytes 49156 | tf_op jit(solution)/shard_map/while
  107.9 4.2 copy-start.3
  120.4 4.0 copy-start.14
  120.4 4.4 copy-start.7
  120.4 4.4 copy-start.17
  131.5 6.7 %copy-start.12 = (f32[128,64]{0,1:T(8,128)S(1)}, f32[128,64]{0,1:T(8,128)}, u32[]{:S(2)}) copy-start(f32[128,64]{0,1:T(8,128)} %get-tuple-element.372) | copy-start | bytes 98308 | tf_op jit(solution)/shard_map/while
  131.5 6.9 %copy-start.11 = (bf16[128,64]{0,1:T(8,128)(2,1)S(1)}, bf16[128,64]{0,1:T(8,128)(2,1)}, u32[]{:S(2)}) copy-start(bf16[128,64]{0,1:T(8,128)(2,1)} %get-tuple-element.400) | copy-start | bytes 49156 | tf_op jit(solution)/shard_map/while
  138.7 4.2 copy-start.3
  151.2 4.4 copy-start.7
  151.3 4.4 copy-start.17
  162.3 6.7 %copy-start.12 = (f32[128,64]{0,1:T(8,128)S(1)}, f32[128,64]{0,1:T(8,128)}, u32[]{:S(2)}) copy-start(f32[128,64]{0,1:T(8,128)} %get-tuple-element.372) | copy-start | bytes 98308 | tf_op jit(solution)/shard_map/while
  162.3 6.9 %copy-start.11 = (bf16[128,64]{0,1:T(8,128)(2,1)S(1)}, bf16[128,64]{0,1:T(8,128)(2,1)}, u32[]{:S(2)}) copy-start(bf16[128,64]{0,1:T(8,128)(2,1)} %get-tuple-element.400) | copy-start | bytes 49156 | tf_op jit(solution)/shard_map/while
  169.5 4.2 copy-start.3
  182.0 4.4 copy-start.7
  182.1 4.4 copy-start.17
  193.0 6.7 %copy-start.12 = (f32[128,64]{0,1:T(8,128)S(1)}, f32[128,64]{0,1:T(8,128)}, u32[]{:S(2)}) copy-start(f32[128,64]{0,1:T(8,128)} %get-tuple-element.372) | copy-start | bytes 98308 | tf_op jit(solution)/shard_map/while
  193.0 6.9 %copy-start.11 = (bf16[128,64]{0,1:T(8,128)(2,1)S(1)}, bf16[128,64]{0,1:T(8,128)(2,1)}, u32[]{:S(2)}) copy-start(bf16[128,64]{0,1:T(8,128)(2,1)} %get-tuple-element.400) | copy-start | bytes 49156 | tf_op jit(solution)/shard_map/while
  200.3 4.2 copy-start.3
  212.8 4.4 copy-start.7
  212.8 4.4 copy-start.17
  223.8 6.7 %copy-start.12 = (f32[128,64]{0,1:T(8,128)S(1)}, f32[128,64]{0,1:T(8,128)}, u32[]{:S(2)}) copy-start(f32[128,64]{0,1:T(8,128)} %get-tuple-element.372) | copy-start | bytes 98308 | tf_op jit(solution)/shard_map/while
  223.8 6.9 %copy-start.11 = (bf16[128,64]{0,1:T(8,128)(2,1)S(1)}, bf16[128,64]{0,1:T(8,128)(2,1)}, u32[]{:S(2)}) copy-start(bf16[128,64]{0,1:T(8,128)(2,1)} %get-tuple-element.400) | copy-start | bytes 49156 | tf_op jit(solution)/shard_map/while
  231.1 4.2 copy-start.3
  243.6 4.4 copy-start.7
  243.6 4.4 copy-start.17
  254.6 6.7 %copy-start.12 = (f32[128,64]{0,1:T(8,128)S(1)}, f32[128,64]{0,1:T(8,128)}, u32[]{:S(2)}) copy-start(f32[128,64]{0,1:T(8,128)} %get-tuple-element.372) | copy-start | bytes 98308 | tf_op jit(solution)/shard_map/while
  254.6 6.9 %copy-start.11 = (bf16[128,64]{0,1:T(8,128)(2,1)S(1)}, bf16[128,64]{0,1:T(8,128)(2,1)}, u32[]{:S(2)}) copy-start(bf16[128,64]{0,1:T(8,128)(2,1)} %get-tuple-element.400) | copy-start | bytes 49156 | tf_op jit(solution)/shard_map/while
  261.9 4.2 copy-start.3
  274.4 4.4 copy-start.7
  274.4 4.4 copy-start.17
  285.4 6.7 %copy-start.12 = (f32[128,64]{0,1:T(8,128)S(1)}, f32[128,64]{0,1:T(8,128)}, u32[]{:S(2)}) copy-start(f32[128,64]{0,1:T(8,128)} %get-tuple-element.372) | copy-start | bytes 98308 | tf_op jit(solution)/shard_map/while
  285.4 6.9 %copy-start.11 = (bf16[128,64]{0,1:T(8,128)(2,1)S(1)}, bf16[128,64]{0,1:T(8,128)(2,1)}, u32[]{:S(2)}) copy-start(bf16[128,64]{0,1:T(8,128)(2,1)} %get-tuple-element.400) | copy-start | bytes 49156 | tf_op jit(solution)/shard_map/while
  292.6 4.2 copy-start.3
  305.2 4.4 copy-start.7
  305.2 4.4 copy-start.17
  316.2 6.7 %copy-start.12 = (f32[128,64]{0,1:T(8,128)S(1)}, f32[128,64]{0,1:T(8,128)}, u32[]{:S(2)}) copy-start(f32[128,64]{0,1:T(8,128)} %get-tuple-element.372) | copy-start | bytes 98308 | tf_op jit(solution)/shard_map/while
  316.2 6.9 %copy-start.11 = (bf16[128,64]{0,1:T(8,128)(2,1)S(1)}, bf16[128,64]{0,1:T(8,128)(2,1)}, u32[]{:S(2)}) copy-start(bf16[128,64]{0,1:T(8,128)(2,1)} %get-tuple-element.400) | copy-start | bytes 49156 | tf_op jit(solution)/shard_map/while
  323.4 4.2 copy-start.3
  335.9 4.4 copy-start.7
  336.0 4.4 copy-start.17
  346.9 6.7 %copy-start.12 = (f32[128,64]{0,1:T(8,128)S(1)}, f32[128,64]{0,1:T(8,128)}, u32[]{:S(2)}) copy-start(f32[128,64]{0,1:T(8,128)} %get-tuple-element.372) | copy-start | bytes 98308 | tf_op jit(solution)/shard_map/while
  346.9 6.9 %copy-start.11 = (bf16[128,64]{0,1:T(8,128)(2,1)S(1)}, bf16[128,64]{0,1:T(8,128)(2,1)}, u32[]{:S(2)}) copy-start(bf16[128,64]{0,1:T(8,128)(2,1)} %get-tuple-element.400) | copy-start | bytes 49156 | tf_op jit(solution)/shard_map/while
  354.2 4.2 copy-start.3
  366.7 4.4 copy-start.7
  366.7 4.4 copy-start.17
  377.7 6.7 %copy-start.12 = (f32[128,64]{0,1:T(8,128)S(1)}, f32[128,64]{0,1:T(8,128)}, u32[]{:S(2)}) copy-start(f32[128,64]{0,1:T(8,128)} %get-tuple-element.372) | copy-start | bytes 98308 | tf_op jit(solution)/shard_map/while
  377.7 6.9 %copy-start.11 = (bf16[128,64]{0,1:T(8,128)(2,1)S(1)}, bf16[128,64]{0,1:T(8,128)(2,1)}, u32[]{:S(2)}) copy-start(bf16[128,64]{0,1:T(8,128)(2,1)} %get-tuple-element.400) | copy-start | bytes 49156 | tf_op jit(solution)/shard_map/while
  385.0 4.2 copy-start.3
  397.5 4.4 copy-start.7
  397.5 4.4 copy-start.17
  408.5 6.7 %copy-start.12 = (f32[128,64]{0,1:T(8,128)S(1)}, f32[128,64]{0,1:T(8,128)}, u32[]{:S(2)}) copy-start(f32[128,64]{0,1:T(8,128)} %get-tuple-element.372) | copy-start | bytes 98308 | tf_op jit(solution)/shard_map/while
  408.5 6.9 %copy-start.11 = (bf16[128,64]{0,1:T(8,128)(2,1)S(1)}, bf16[128,64]{0,1:T(8,128)(2,1)}, u32[]{:S(2)}) copy-start(bf16[128,64]{0,1:T(8,128)(2,1)} %get-tuple-element.400) | copy-start | bytes 49156 | tf_op jit(solution)/shard_map/while
  415.8 4.2 copy-start.3
  424.5 129.1 %reduce-scatter.4.cloned.1.call-start = ((), (), s32[]{:S(2)}) async-start(), calls=%async_computation.2 | async-start | bytes 61440
  425.1 198.3 %all-reduce.5.cloned.1.call-start = ((), (), s32[]{:S(2)}) async-start(), calls=%async_computation.1 | async-start | bytes 196608 | tf_op jit(solution)/shard_map/psum | solution.py:113
  (144 other events, 347.9 us)
Sparse Core Ops, SparseCore 0:
  424.7 125.5 all-reduce.6
  554.2 69.1 all-reduce.4
Sparse Core Ops, SparseCore 1:
  428.0 15.6 reduce-scatter.3
where the time goes:
time: 636 us; the launch traced here: 632 us
  matrix products  222 us (35%)
  waiting for transfers between devices  158 us (25%)
  local copies, waits for them, and re-layouts  85.1 us (13%)
  blocking collectives  81.5 us (13%)
  other arithmetic  65.9 us (10%)
  between operations  15.5 us (2%)
    psum x1, waiting for transfers between devices, on_device(): lax.psum((running[0], running[1], running[2]), ('row', 'col'))  86.6 us
    psum x1, waiting for transfers between devices, on_device(): grad_right = lax.psum(running[3], 'row')  69.8 us
    div x12, matrix products, pair_backward(): probs = expo / jnp.sum(expo, axis=-1, keepdims=True)  60.6 us
    dot_general x36, matrix products, outer(): lax.dot_general(first, second, (((1,), (1,)), ((), ())), preferred_elemen...  57.6 us
    dot_general x24, matrix products, transition(): jnp.dot(hidden, w_out, preferred_element_type=jnp.float32)  45.4 us
    all_gather x1, blocking collectives, on_device(): everything = lax.all_gather(stacked, ('row', 'col'), axis=1, tiled=True)  44.3 us
    psum x1, blocking collectives, on_device(): lax.psum((running[0], running[1], running[2]), ('row', 'col'))  37.2 us
    dot_general x12, matrix products, transition(): pre_act = jnp.dot(normed, w_in, preferred_element_type=jnp.float32) + b_in  30.8 us
  transfers between devices with their start and end apart: 3, of which 2 were waited for; matrix products, arithmetic and copies ran while one was open for 1% of the time, Pallas kernels for 0%

commit v1 on v0

--- a/solution.py
+++ b/solution.py
@@ -110,7 +110,9 @@
     grad_left = lax.psum_scatter(
         left_terms.reshape(tile_rows, width), "col", scatter_dimension=0, tiled=True
     )
-    grad_right = lax.psum(running[3], "row")
+    part = running[3]
+    pieces = lax.all_gather(part, "row")
+    grad_right = jnp.sum(pieces, axis=0)
     grad_in, grad_out, grad_bins = lax.psum((running[0], running[1], running[2]), ("row", "col"))
     residues = tile_rows * lax.axis_size("row")
     return (grad_left, grad_right, grad_in / residues, grad_out / residues, grad_bins / residues)

time: 636 us -> 565 us (0.89)
  waiting for transfers between devices: 158 us -> 54.4 us
  blocking collectives: 81.5 us -> 114 us
    psum x1 -> x0, waiting for transfers between devices: 69.8 us -> none  [on_device(): grad_right = lax.psum(running[3], 'row')]
    psum x1, waiting for transfers between devices: 86.6 us -> 53.8 us  [on_device(): lax.psum((running[0], running[1], running[2]), ('row', 'col'))]
    all_gather x0 -> x1, blocking collectives: none -> 32.7 us  [on_device(): pieces = lax.all_gather(part, 'row')]
  transfers between devices with their start and end apart: 3 -> 2, of which waited for: 2 -> 1; matrix products, arithmetic and copies ran while one was open for 1% -> 1% of each run, Pallas kernels for 0% -> 0%
where the time goes in v1:
time: 565 us; the launch traced here: 561 us
  matrix products  222 us (39%)
  blocking collectives  114 us (20%)
  local copies, waits for them, and re-layouts  83.5 us (15%)
  other arithmetic  66.6 us (12%)
  waiting for transfers between devices  54.4 us (10%)
  between operations  15.5 us (3%)
    div x12, matrix products, pair_backward(): probs = expo / jnp.sum(expo, axis=-1, keepdims=True)  60.6 us
    dot_general x36, matrix products, outer(): lax.dot_general(first, second, (((1,), (1,)), ((), ())), preferred_elemen...  57.6 us
    psum x1, waiting for transfers between devices, on_device(): lax.psum((running[0], running[1], running[2]), ('row', 'col'))  53.8 us
    dot_general x24, matrix products, transition(): jnp.dot(hidden, w_out, preferred_element_type=jnp.float32)  45.4 us
    all_gather x1, blocking collectives, on_device(): everything = lax.all_gather(stacked, ('row', 'col'), axis=1, tiled=True)  44.3 us
    psum x1, blocking collectives, on_device(): lax.psum((running[0], running[1], running[2]), ('row', 'col'))  37.3 us
    all_gather x1, blocking collectives, on_device(): pieces = lax.all_gather(part, 'row')  32.7 us
    dot_general x12, matrix products, transition(): pre_act = jnp.dot(normed, w_in, preferred_element_type=jnp.float32) + b_in  30.8 us
  transfers between devices with their start and end apart: 2, of which 1 were waited for; matrix products, arithmetic and copies ran while one was open for 1% of the time, Pallas kernels for 0%

profile of v1, /device:TPU:0, one launch (start us, length us, event | category | flops | bytes accessed | tf_op | source)
XLA Modules:
  0.0 561.1 jit_solution(12517910260999612318)
XLA Ops:
  8.8 44.3 %all_gather.9 = bf16[2,768,128]{2,1,0:T(8,128)(2,1)S(1)} all-gather(bf16[2,24,128]{2,1,0:T(8,128)(2,1)S(1)} %pad_maximum_fusion), channel_id=1, replica_groups=mesh['row'=8,'col'=4] {'row','col'}, dimensions={1}, use_global_device_ids=true | all-gather | bytes 405504 | tf_op jit(solution)/shard_map/all_gather | solution.py:67
  54.4 369.4 %while.19 = (s32[]{:T(128)}, f32[128,512]{1,0:T(8,128)}, f32[512,128]{1,0:T(8,128)S(1)}, f32[128,64]{0,1:T(8,128)}, f32[192,128]{1,0:T(8,128)}, /*index=5*/f32[1...) while((s32[]{:T(128)}, f32[128,512]{1,0:T(8,128)}, ...), condition=%wide.region_11.12_spmd.clone, body=%wide.region_0.11_spmd.clone.sunk | while | flops 1737784448 | bytes 44289180 | solution.py:109
  58.9 3.2 fusion.120
  63.3 2.6 multiply_convert_fusion.3
  69.9 5.1 fusion.121
  77.1 3.5 fusion.123
  89.7 3.2 fusion.120
  94.1 2.6 multiply_convert_fusion.3
  100.7 5.1 fusion.121
  105.7 1.4 copy.32
  107.9 3.5 fusion.123
  120.5 3.2 fusion.120
  124.9 2.6 multiply_convert_fusion.3
  131.5 5.1 fusion.121
  136.5 1.4 copy.32
  138.7 3.5 fusion.123
  151.3 3.2 fusion.120
  155.7 2.6 multiply_convert_fusion.3
  162.3 5.1 fusion.121
  167.3 1.4 copy.32
  169.5 3.5 fusion.123
  182.1 3.2 fusion.120
  186.5 2.6 multiply_convert_fusion.3
  193.0 5.1 fusion.121
  198.1 1.4 copy.32
  200.3 3.5 fusion.123
  212.8 3.2 fusion.120
  217.3 2.6 multiply_convert_fusion.3
  223.8 5.1 fusion.121
  228.9 1.4 copy.32
  231.1 3.5 fusion.123
  243.6 3.2 fusion.120
  248.1 2.6 multiply_convert_fusion.3
  254.6 5.1 fusion.121
  259.7 1.4 copy.32
  261.9 3.5 fusion.123
  274.4 3.2 fusion.120
  278.9 2.6 multiply_convert_fusion.3
  285.4 5.1 fusion.121
  292.6 3.5 fusion.123
  305.2 3.2 fusion.120
  309.6 2.6 multiply_convert_fusion.3
  316.2 5.1 fusion.121
  321.2 1.4 copy.32
  323.4 3.5 fusion.123
  336.0 3.2 fusion.120
  340.4 2.6 multiply_convert_fusion.3
  346.9 5.1 fusion.121
  352.0 1.4 copy.32
  354.2 3.5 fusion.123
  366.7 3.2 fusion.120
  371.2 2.6 multiply_convert_fusion.3
  377.7 5.1 fusion.121
  385.0 3.5 fusion.123
  397.5 3.2 fusion.120
  402.0 2.6 multiply_convert_fusion.3
  408.5 5.1 fusion.121
  413.6 1.4 copy.32
  415.8 3.5 fusion.123
  425.1 37.3 %psum.23 = f32[128,64]{0,1:T(8,128)S(1)} all-reduce(f32[128,64]{0,1:T(8,128)} %get-tuple-element.95), channel_id=1, replica_groups=mesh['row'=8,'col'=4] {'row','col'}, use_global_device_ids=true, to_apply=%region_16.17 | all-reduce | flops 8192 | bytes 65536 | tf_op jit(solution)/shard_map/psum | solution.py:116
  463.0 32.7 %all-gather = f32[1536,128]{1,0:T(8,128)S(1)} all-gather(f32[192,128]{1,0:T(8,128)} %get-tuple-element.92), channel_id=2, replica_groups=mesh['row'=8,'col'=4] {'row'}, dimensions={0}, use_global_device_ids=true | all-gather | bytes 884736 | tf_op jit(solution)/shard_map/all_gather | solution.py:114
  496.5 53.8 %all-reduce.4.cloned.1.call-done = (f32[128,512]{1,0:T(8,128)}, f32[512,128]{1,0:T(8,128)}) async-done(((f32[128,512]{1,0:T(8,128)}, f32[512,128]{1,0:T(8,128)}), (f32[128,512]{1,0:T(8,128)}, f32[512,128]{1,0:T(8,128)})) %all-reduce.4.cloned.1.call-update) | async-done | bytes 524304 | tf_op jit(solution)/shard_map/psum | solution.py:116
  550.3 1.7 broadcast_multiply_fusion.5
  552.0 1.7 broadcast_multiply_fusion.4
  (824 shorter events, 184.6 us)
Async XLA Ops:
  8.0 542.3 %all-reduce.4.cloned.1.call-start = ((), (), s32[]{:S(2)}) async-start(), calls=%async_computation.2 | async-start | bytes 1048576 | tf_op jit(solution)/shard_map/psum | solution.py:116
  58.9 4.4 copy-start.7
  58.9 4.4 copy-start.17
  69.9 6.7 %copy-start.12 = (f32[128,64]{0,1:T(8,128)S(1)}, f32[128,64]{0,1:T(8,128)}, u32[]{:S(2)}) copy-start(f32[128,64]{0,1:T(8,128)} %get-tuple-element.372) | copy-start | bytes 98308 | tf_op jit(solution)/shard_map/while
  69.9 6.9 %copy-start.11 = (bf16[128,64]{0,1:T(8,128)(2,1)S(1)}, bf16[128,64]{0,1:T(8,128)(2,1)}, u32[]{:S(2)}) copy-start(bf16[128,64]{0,1:T(8,128)(2,1)} %get-tuple-element.400) | copy-start | bytes 49156 | tf_op jit(solution)/shard_map/while
  77.1 4.2 copy-start.3
  89.6 4.4 copy-start.7
  89.7 4.4 copy-start.17
  100.6 6.7 %copy-start.12 = (f32[128,64]{0,1:T(8,128)S(1)}, f32[128,64]{0,1:T(8,128)}, u32[]{:S(2)}) copy-start(f32[128,64]{0,1:T(8,128)} %get-tuple-element.372) | copy-start | bytes 98308 | tf_op jit(solution)/shard_map/while
  100.7 6.9 %copy-start.11 = (bf16[128,64]{0,1:T(8,128)(2,1)S(1)}, bf16[128,64]{0,1:T(8,128)(2,1)}, u32[]{:S(2)}) copy-start(bf16[128,64]{0,1:T(8,128)(2,1)} %get-tuple-element.400) | copy-start | bytes 49156 | tf_op jit(solution)/shard_map/while
  107.9 4.2 copy-start.3
  120.4 4.0 copy-start.14
  120.4 4.4 copy-start.7
  120.4 4.4 copy-start.17
  131.5 6.7 %copy-start.12 = (f32[128,64]{0,1:T(8,128)S(1)}, f32[128,64]{0,1:T(8,128)}, u32[]{:S(2)}) copy-start(f32[128,64]{0,1:T(8,128)} %get-tuple-element.372) | copy-start | bytes 98308 | tf_op jit(solution)/shard_map/while
  131.5 6.9 %copy-start.11 = (bf16[128,64]{0,1:T(8,128)(2,1)S(1)}, bf16[128,64]{0,1:T(8,128)(2,1)}, u32[]{:S(2)}) copy-start(bf16[128,64]{0,1:T(8,128)(2,1)} %get-tuple-element.400) | copy-start | bytes 49156 | tf_op jit(solution)/shard_map/while
  138.7 4.2 copy-start.3
  151.2 4.0 copy-start.14
  151.2 4.4 copy-start.7
  151.3 4.4 copy-start.17
  162.3 6.7 %copy-start.12 = (f32[128,64]{0,1:T(8,128)S(1)}, f32[128,64]{0,1:T(8,128)}, u32[]{:S(2)}) copy-start(f32[128,64]{0,1:T(8,128)} %get-tuple-element.372) | copy-start | bytes 98308 | tf_op jit(solution)/shard_map/while
  162.3 6.9 %copy-start.11 = (bf16[128,64]{0,1:T(8,128)(2,1)S(1)}, bf16[128,64]{0,1:T(8,128)(2,1)}, u32[]{:S(2)}) copy-start(bf16[128,64]{0,1:T(8,128)(2,1)} %get-tuple-element.400) | copy-start | bytes 49156 | tf_op jit(solution)/shard_map/while
  169.5 4.2 copy-start.3
  182.0 4.4 copy-start.7
  182.1 4.4 copy-start.17
  193.0 6.7 %copy-start.12 = (f32[128,64]{0,1:T(8,128)S(1)}, f32[128,64]{0,1:T(8,128)}, u32[]{:S(2)}) copy-start(f32[128,64]{0,1:T(8,128)} %get-tuple-element.372) | copy-start | bytes 98308 | tf_op jit(solution)/shard_map/while
  193.0 6.9 %copy-start.11 = (bf16[128,64]{0,1:T(8,128)(2,1)S(1)}, bf16[128,64]{0,1:T(8,128)(2,1)}, u32[]{:S(2)}) copy-start(bf16[128,64]{0,1:T(8,128)(2,1)} %get-tuple-element.400) | copy-start | bytes 49156 | tf_op jit(solution)/shard_map/while
  200.3 4.2 copy-start.3
  212.8 4.4 copy-start.7
  212.8 4.4 copy-start.17
  223.8 6.7 %copy-start.12 = (f32[128,64]{0,1:T(8,128)S(1)}, f32[128,64]{0,1:T(8,128)}, u32[]{:S(2)}) copy-start(f32[128,64]{0,1:T(8,128)} %get-tuple-element.372) | copy-start | bytes 98308 | tf_op jit(solution)/shard_map/while
  223.8 6.9 %copy-start.11 = (bf16[128,64]{0,1:T(8,128)(2,1)S(1)}, bf16[128,64]{0,1:T(8,128)(2,1)}, u32[]{:S(2)}) copy-start(bf16[128,64]{0,1:T(8,128)(2,1)} %get-tuple-element.400) | copy-start | bytes 49156 | tf_op jit(solution)/shard_map/while
  231.1 4.2 copy-start.3
  243.6 4.4 copy-start.7
  243.6 4.4 copy-start.17
  254.6 6.7 %copy-start.12 = (f32[128,64]{0,1:T(8,128)S(1)}, f32[128,64]{0,1:T(8,128)}, u32[]{:S(2)}) copy-start(f32[128,64]{0,1:T(8,128)} %get-tuple-element.372) | copy-start | bytes 98308 | tf_op jit(solution)/shard_map/while
  254.6 6.9 %copy-start.11 = (bf16[128,64]{0,1:T(8,128)(2,1)S(1)}, bf16[128,64]{0,1:T(8,128)(2,1)}, u32[]{:S(2)}) copy-start(bf16[128,64]{0,1:T(8,128)(2,1)} %get-tuple-element.400) | copy-start | bytes 49156 | tf_op jit(solution)/shard_map/while
  261.9 4.2 copy-start.3
  274.4 4.4 copy-start.7
  274.4 4.4 copy-start.17
  285.4 6.7 %copy-start.12 = (f32[128,64]{0,1:T(8,128)S(1)}, f32[128,64]{0,1:T(8,128)}, u32[]{:S(2)}) copy-start(f32[128,64]{0,1:T(8,128)} %get-tuple-element.372) | copy-start | bytes 98308 | tf_op jit(solution)/shard_map/while
  285.4 6.9 %copy-start.11 = (bf16[128,64]{0,1:T(8,128)(2,1)S(1)}, bf16[128,64]{0,1:T(8,128)(2,1)}, u32[]{:S(2)}) copy-start(bf16[128,64]{0,1:T(8,128)(2,1)} %get-tuple-element.400) | copy-start | bytes 49156 | tf_op jit(solution)/shard_map/while
  292.6 4.2 copy-start.3
  305.2 4.4 copy-start.7
  305.2 4.4 copy-start.17
  316.2 6.7 %copy-start.12 = (f32[128,64]{0,1:T(8,128)S(1)}, f32[128,64]{0,1:T(8,128)}, u32[]{:S(2)}) copy-start(f32[128,64]{0,1:T(8,128)} %get-tuple-element.372) | copy-start | bytes 98308 | tf_op jit(solution)/shard_map/while
  316.2 6.9 %copy-start.11 = (bf16[128,64]{0,1:T(8,128)(2,1)S(1)}, bf16[128,64]{0,1:T(8,128)(2,1)}, u32[]{:S(2)}) copy-start(bf16[128,64]{0,1:T(8,128)(2,1)} %get-tuple-element.400) | copy-start | bytes 49156 | tf_op jit(solution)/shard_map/while
  323.4 4.2 copy-start.3
  335.9 4.4 copy-start.7
  336.0 4.4 copy-start.17
  346.9 6.7 %copy-start.12 = (f32[128,64]{0,1:T(8,128)S(1)}, f32[128,64]{0,1:T(8,128)}, u32[]{:S(2)}) copy-start(f32[128,64]{0,1:T(8,128)} %get-tuple-element.372) | copy-start | bytes 98308 | tf_op jit(solution)/shard_map/while
  346.9 6.9 %copy-start.11 = (bf16[128,64]{0,1:T(8,128)(2,1)S(1)}, bf16[128,64]{0,1:T(8,128)(2,1)}, u32[]{:S(2)}) copy-start(bf16[128,64]{0,1:T(8,128)(2,1)} %get-tuple-element.400) | copy-start | bytes 49156 | tf_op jit(solution)/shard_map/while
  354.2 4.2 copy-start.3
  366.7 4.4 copy-start.7
  366.7 4.4 copy-start.17
  377.7 6.7 %copy-start.12 = (f32[128,64]{0,1:T(8,128)S(1)}, f32[128,64]{0,1:T(8,128)}, u32[]{:S(2)}) copy-start(f32[128,64]{0,1:T(8,128)} %get-tuple-element.372) | copy-start | bytes 98308 | tf_op jit(solution)/shard_map/while
  377.7 6.9 %copy-start.11 = (bf16[128,64]{0,1:T(8,128)(2,1)S(1)}, bf16[128,64]{0,1:T(8,128)(2,1)}, u32[]{:S(2)}) copy-start(bf16[128,64]{0,1:T(8,128)(2,1)} %get-tuple-element.400) | copy-start | bytes 49156 | tf_op jit(solution)/shard_map/while
  385.0 4.2 copy-start.3
  397.5 4.4 copy-start.7
  397.5 4.4 copy-start.17
  408.5 6.7 %copy-start.12 = (f32[128,64]{0,1:T(8,128)S(1)}, f32[128,64]{0,1:T(8,128)}, u32[]{:S(2)}) copy-start(f32[128,64]{0,1:T(8,128)} %get-tuple-element.372) | copy-start | bytes 98308 | tf_op jit(solution)/shard_map/while
  408.5 6.9 %copy-start.11 = (bf16[128,64]{0,1:T(8,128)(2,1)S(1)}, bf16[128,64]{0,1:T(8,128)(2,1)}, u32[]{:S(2)}) copy-start(bf16[128,64]{0,1:T(8,128)(2,1)} %get-tuple-element.400) | copy-start | bytes 49156 | tf_op jit(solution)/shard_map/while
  415.8 4.2 copy-start.3
  424.5 129.1 %reduce-scatter.4.cloned.1.call-start = ((), (), s32[]{:S(2)}) async-start(), calls=%async_computation.1 | async-start | bytes 61440
  (143 other events, 343.9 us)
Sparse Core Ops, SparseCore 0:
  424.7 125.5 all-reduce.3
Sparse Core Ops, SparseCore 1:
  428.0 15.6 reduce-scatter.3
